TPU v7x, 32 devices: a whole 2x2x4 slice. The times are simulated.
32 devices in a mesh: site: 4 (over y, x), bond: 8 (over z, core).
Axes of the slice: x: 2, y: 2, z: 4, core: 2. Of those that a mesh axis runs over, the one named last changes fastest.
Arguments:
- start_rows: bfloat16 [1024, 4096], P(None, 'bond'), may hold values from -6 to 6
- site_tensors: bfloat16 [4, 4096, 8, 4096], P('site', None, None, 'bond'), may hold values from -0.09375 to 0.09375
- block_scales: float32 [4, 8, 32], P('site', None, 'bond'), may hold values from 0.25 to 1
- displacement: float32 [4, 8, 8], P('site'), may hold values from -0.9 to 0.9
- outcomes: int32 [4, 1024], P('site'), may hold values from 0 to 7
Outputs:
- leaving: bfloat16 [4, 1024, 4096], P('site', None, 'bond')
- log_norms: float32 [4, 1024], P('site')
Inputs may be any that keep to these rules, and one draw needn't show every extreme that they name: outcomes index the second dimension of displacement.
All inputs are finite; a program needn't handle non-finite values.
Results may differ from a plain program's by a relative error of at most 0.014.
Values may be sent and summed in bfloat16 or wider, within the bound.
A program may use at most 128 MiB of HBM per device.

v0:
```python
import jax
import jax.numpy as jnp
from jax import lax
from jax.sharding import PartitionSpec as P

ROWS = 512


def shifted(value, axis, steps):
    count = lax.axis_size(axis)
    initial, last = (max(0, -steps), min(count, count - steps))
    return lax.ppermute(value, axis, [(source, source + steps) for source in range(initial, last)])


def local(start_rows, site_tensors, block_scales, displacement, outcomes):
    sites = lax.axis_size("site")
    cols = site_tensors.shape[3]
    chi = site_tensors.shape[1]
    phys = site_tensors.shape[2]
    nblk = block_scales.shape[2]
    allrows = start_rows.shape[0]
    grows = ROWS
    ngroups = allrows // grows
    ticks = ngroups + sites - 1
    a_mat = site_tensors[0].reshape(chi, phys * cols)
    scales = block_scales[0][:, :, None]
    table = displacement[0]
    outcome_row = outcomes[0]
    position = lax.axis_index("site")

    def tick(step, carry):
        incoming, incoming_norm, out_leave, out_logs = carry
        batch = step - position
        valid = jnp.logical_and(batch >= 0, batch < ngroups)
        first = jnp.clip(batch, 0, ngroups - 1) * grows
        start_piece = lax.dynamic_slice_in_dim(start_rows, first, grows, 0)
        rows_in = jnp.where(position == 0, start_piece, incoming)
        piece = lax.all_gather(rows_in, "bond", axis=1, tiled=True)
        total = jnp.dot(piece, a_mat, preferred_element_type=jnp.float32)
        pf = piece.astype(jnp.float32)
        total, squares = (total, jnp.sum(pf * pf, axis=1))
        local_norm = jnp.sqrt(squares / chi + 1e-06)
        prod = total.reshape(grows, phys, nblk, cols // nblk) * scales[None]
        prod = prod.reshape(grows, phys, cols)
        picked = lax.dynamic_slice_in_dim(outcome_row, first, grows, 0)
        onehot = (picked[:, None] == jnp.arange(phys, dtype=jnp.int32)[None, :]).astype(jnp.float32)
        weight = jnp.dot(onehot, table, precision=lax.Precision.HIGHEST)
        mixed = jnp.sum(weight[:, :, None] * prod, axis=1)
        leave = (mixed / local_norm[:, None]).astype(jnp.bfloat16)
        out_leave = jnp.where(
            valid, lax.dynamic_update_slice_in_dim(out_leave, leave, first, 0), out_leave
        )
        out_logs = jnp.where(
            valid,
            lax.dynamic_update_slice_in_dim(out_logs, jnp.log(local_norm), first, 0),
            out_logs,
        )
        incoming = shifted(leave, "site", 1)
        return (incoming, incoming_norm, out_leave, out_logs)

    carry = (
        jnp.zeros((grows, cols), jnp.bfloat16),
        jnp.ones((grows,), jnp.float32),
        jnp.zeros((allrows, cols), jnp.bfloat16),
        jnp.zeros((allrows,), jnp.float32),
    )
    carry = lax.fori_loop(0, ticks, tick, carry)
    return (carry[2][None], carry[3][None])


def solution(mesh):
    return jax.shard_map(
        local,
        mesh=mesh,
        in_specs=(
            P(None, "bond"),
            P("site", None, None, "bond"),
            P("site", None, "bond"),
            P("site", None, None),
            P("site", None),
        ),
        out_specs=(P("site", None, "bond"), P("site", None)),
        check_vma=False,
    )
```

profile of v0, /device:TPU:4, one launch (start us, length us, event | category | flops | bytes accessed | tf_op | source)
XLA Modules:
  0.0 550.5 jit_solution(6089565585654436752)
XLA Ops:
  7.2 22.7 %copy.10 = bf16[512,8,8,512]{3,1,2,0:T(8,128)(2,1)} copy(bf16[512,8,8,512]{3,2,1,0:T(8,128)(2,1)} %bitcast.35) | data formatting | bytes 67108864
  31.1 512.3 %while.18 = (s32[]{:T(128)}, bf16[512,512]{1,0:T(8,128)(2,1)S(1)}, bf16[1024,512]{1,0:T(8,128)(2,1)}, f32[1024]{0:T(1024)S(1)}, s32[]{:T(128)}, /*index=5*/s32[1...) while((s32[]{:T(128)}, bf16[512,512]{1,0:T(8,128)(2,1)S(1)}, ...), condition=%wide.region_3.4_spmd, body=%wide.region_0.3_spmd.sunk | while | flops 17193637888 | bytes 113855224 | solution.py:67
  33.6 47.9 %all-gather.2.cloned.1.call-done = bf16[512,4096]{1,0:T(8,128)(2,1)} async-done(((bf16[512,512]{1,0:T(8,128)(2,1)}), bf16[512,4096]{1,0:T(8,128)(2,1)}) %all-gather.2.cloned.1.call-update) | async-done | bytes 4194320 | tf_op jit(solution)/shard_map/while/body/eval_jaxpr/all_gather | solution.py:38
  81.6 22.6 %fusion.18 = f32[512,4096]{1,0:T(8,128)S(1)} fusion(bf16[512,4096]{1,0:T(8,128)(2,1)} %all-gather.2.cloned.1.call-done, bf16[4096,4096]{1,0:T(8,128)(2,1)} %get-tuple-element.361), kind=kOutput, calls=%fused_computation.14.clone.1 | convolution fusion | flops 17179869184 | bytes 46137344 | tf_op jit(solution)/shard_map/while/body/eval_jaxpr/dot_general | solution.py:39
  104.2 8.2 %copy.12 = f32[64,8,8,512]{3,2,1,0:T(8,128)S(1)} copy(f32[64,8,8,512]{3,1,2,0:T(8,128)S(1)} %bitcast.34) | data formatting | bytes 16777216 | tf_op jit(solution)/shard_map/while
  113.5 3.9 fusion.20
  119.4 3.4 collective-permute-start
  122.8 13.5 %collective-permute-done = bf16[512,512]{1,0:T(8,128)(2,1)S(1)} collective-permute-done((bf16[512,512]{1,0:T(8,128)(2,1)S(1)}, bf16[512,512]{1,0:T(8,128)(2,1)S(1)}, u32[]{:S(2)}, u32[]{:S(2)}) %collective-permute-start) | collective-permute-done | bytes 524320 | tf_op jit(solution)/shard_map/while/body/eval_jaxpr/ppermute | solution.py:12
  138.8 44.7 %all-gather.2.cloned.1.call-done = bf16[512,4096]{1,0:T(8,128)(2,1)} async-done(((bf16[512,512]{1,0:T(8,128)(2,1)}), bf16[512,4096]{1,0:T(8,128)(2,1)}) %all-gather.2.cloned.1.call-update) | async-done | bytes 4194320 | tf_op jit(solution)/shard_map/while/body/eval_jaxpr/all_gather | solution.py:38
  183.5 22.6 %fusion.18 = f32[512,4096]{1,0:T(8,128)S(1)} fusion(bf16[512,4096]{1,0:T(8,128)(2,1)} %all-gather.2.cloned.1.call-done, bf16[4096,4096]{1,0:T(8,128)(2,1)} %get-tuple-element.361), kind=kOutput, calls=%fused_computation.14.clone.1 | convolution fusion | flops 17179869184 | bytes 46137344 | tf_op jit(solution)/shard_map/while/body/eval_jaxpr/dot_general | solution.py:39
  206.1 8.2 %copy.12 = f32[64,8,8,512]{3,2,1,0:T(8,128)S(1)} copy(f32[64,8,8,512]{3,1,2,0:T(8,128)S(1)} %bitcast.34) | data formatting | bytes 16777216 | tf_op jit(solution)/shard_map/while
  215.4 3.9 fusion.20
  221.4 3.4 collective-permute-start
  224.7 13.5 %collective-permute-done = bf16[512,512]{1,0:T(8,128)(2,1)S(1)} collective-permute-done((bf16[512,512]{1,0:T(8,128)(2,1)S(1)}, bf16[512,512]{1,0:T(8,128)(2,1)S(1)}, u32[]{:S(2)}, u32[]{:S(2)}) %collective-permute-start) | collective-permute-done | bytes 524320 | tf_op jit(solution)/shard_map/while/body/eval_jaxpr/ppermute | solution.py:12
  240.7 44.7 %all-gather.2.cloned.1.call-done = bf16[512,4096]{1,0:T(8,128)(2,1)} async-done(((bf16[512,512]{1,0:T(8,128)(2,1)}), bf16[512,4096]{1,0:T(8,128)(2,1)}) %all-gather.2.cloned.1.call-update) | async-done | bytes 4194320 | tf_op jit(solution)/shard_map/while/body/eval_jaxpr/all_gather | solution.py:38
  285.4 22.6 %fusion.18 = f32[512,4096]{1,0:T(8,128)S(1)} fusion(bf16[512,4096]{1,0:T(8,128)(2,1)} %all-gather.2.cloned.1.call-done, bf16[4096,4096]{1,0:T(8,128)(2,1)} %get-tuple-element.361), kind=kOutput, calls=%fused_computation.14.clone.1 | convolution fusion | flops 17179869184 | bytes 46137344 | tf_op jit(solution)/shard_map/while/body/eval_jaxpr/dot_general | solution.py:39
  308.0 8.2 %copy.12 = f32[64,8,8,512]{3,2,1,0:T(8,128)S(1)} copy(f32[64,8,8,512]{3,1,2,0:T(8,128)S(1)} %bitcast.34) | data formatting | bytes 16777216 | tf_op jit(solution)/shard_map/while
  317.3 3.9 fusion.20
  323.3 3.4 collective-permute-start
  326.6 13.5 %collective-permute-done = bf16[512,512]{1,0:T(8,128)(2,1)S(1)} collective-permute-done((bf16[512,512]{1,0:T(8,128)(2,1)S(1)}, bf16[512,512]{1,0:T(8,128)(2,1)S(1)}, u32[]{:S(2)}, u32[]{:S(2)}) %collective-permute-start) | collective-permute-done | bytes 524320 | tf_op jit(solution)/shard_map/while/body/eval_jaxpr/ppermute | solution.py:12
  342.6 44.4 %all-gather.2.cloned.1.call-done = bf16[512,4096]{1,0:T(8,128)(2,1)} async-done(((bf16[512,512]{1,0:T(8,128)(2,1)}), bf16[512,4096]{1,0:T(8,128)(2,1)}) %all-gather.2.cloned.1.call-update) | async-done | bytes 4194320 | tf_op jit(solution)/shard_map/while/body/eval_jaxpr/all_gather | solution.py:38
  387.0 22.6 %fusion.18 = f32[512,4096]{1,0:T(8,128)S(1)} fusion(bf16[512,4096]{1,0:T(8,128)(2,1)} %all-gather.2.cloned.1.call-done, bf16[4096,4096]{1,0:T(8,128)(2,1)} %get-tuple-element.361), kind=kOutput, calls=%fused_computation.14.clone.1 | convolution fusion | flops 17179869184 | bytes 46137344 | tf_op jit(solution)/shard_map/while/body/eval_jaxpr/dot_general | solution.py:39
  409.7 8.2 %copy.12 = f32[64,8,8,512]{3,2,1,0:T(8,128)S(1)} copy(f32[64,8,8,512]{3,1,2,0:T(8,128)S(1)} %bitcast.34) | data formatting | bytes 16777216 | tf_op jit(solution)/shard_map/while
  418.9 3.9 fusion.20
  424.9 3.4 collective-permute-start
  428.3 13.5 %collective-permute-done = bf16[512,512]{1,0:T(8,128)(2,1)S(1)} collective-permute-done((bf16[512,512]{1,0:T(8,128)(2,1)S(1)}, bf16[512,512]{1,0:T(8,128)(2,1)S(1)}, u32[]{:S(2)}, u32[]{:S(2)}) %collective-permute-start) | collective-permute-done | bytes 524320 | tf_op jit(solution)/shard_map/while/body/eval_jaxpr/ppermute | solution.py:12
  444.2 44.4 %all-gather.2.cloned.1.call-done = bf16[512,4096]{1,0:T(8,128)(2,1)} async-done(((bf16[512,512]{1,0:T(8,128)(2,1)}), bf16[512,4096]{1,0:T(8,128)(2,1)}) %all-gather.2.cloned.1.call-update) | async-done | bytes 4194320 | tf_op jit(solution)/shard_map/while/body/eval_jaxpr/all_gather | solution.py:38
  488.7 22.6 %fusion.18 = f32[512,4096]{1,0:T(8,128)S(1)} fusion(bf16[512,4096]{1,0:T(8,128)(2,1)} %all-gather.2.cloned.1.call-done, bf16[4096,4096]{1,0:T(8,128)(2,1)} %get-tuple-element.361), kind=kOutput, calls=%fused_computation.14.clone.1 | convolution fusion | flops 17179869184 | bytes 46137344 | tf_op jit(solution)/shard_map/while/body/eval_jaxpr/dot_general | solution.py:39
  511.3 8.2 %copy.12 = f32[64,8,8,512]{3,2,1,0:T(8,128)S(1)} copy(f32[64,8,8,512]{3,1,2,0:T(8,128)S(1)} %bitcast.34) | data formatting | bytes 16777216 | tf_op jit(solution)/shard_map/while
  520.6 3.9 fusion.20
  526.5 3.4 collective-permute-start
  529.9 13.5 %collective-permute-done = bf16[512,512]{1,0:T(8,128)(2,1)S(1)} collective-permute-done((bf16[512,512]{1,0:T(8,128)(2,1)S(1)}, bf16[512,512]{1,0:T(8,128)(2,1)S(1)}, u32[]{:S(2)}, u32[]{:S(2)}) %collective-permute-start) | collective-permute-done | bytes 524320 | tf_op jit(solution)/shard_map/while/body/eval_jaxpr/ppermute | solution.py:12
  (66 shorter events, 29.9 us)
Async XLA Ops:
  7.2 23.9 %copy-start.1 = (f32[1,8,8]{2,1,0:T(8,128)S(1)}, f32[1,8,8]{2,1,0:T(8,128)}, u32[]{:S(2)}) copy-start(f32[1,8,8]{2,1,0:T(8,128)} %param.10) | copy-start | bytes 772
  7.2 23.9 %copy-start.2 = (f32[1,8,4]{1,2,0:T(4,128)S(1)}, f32[1,8,4]{1,2,0:T(4,128)}, u32[]{:S(2)}) copy-start(f32[1,8,4]{1,2,0:T(4,128)} %param.9) | copy-start | bytes 388
  7.2 23.9 %copy-start.4 = (s32[1,1024]{1,0:T(1,128)S(1)}, s32[1,1024]{1,0:T(1,128)}, u32[]{:S(2)}) copy-start(s32[1,1024]{1,0:T(1,128)} %param.11) | copy-start | bytes 12292
  31.1 50.5 %all-gather.2.cloned.1.call-start = ((), (), s32[]{:S(2)}) async-start(), calls=%async_computation | async-start | bytes 4718592 | tf_op jit(solution)/shard_map/while/body/eval_jaxpr/all_gather | solution.py:38
  104.2 8.2 %copy-start = (bf16[512,4096]{1,0:T(8,128)(2,1)S(1)}, bf16[512,4096]{1,0:T(8,128)(2,1)}, u32[]{:S(2)}) copy-start(bf16[512,4096]{1,0:T(8,128)(2,1)} %all-gather.2.cloned.1.call-done) | copy-start | bytes 12582916 | tf_op jit(solution)/shard_map/while
  119.4 16.8 %collective-permute-start = (bf16[512,512]{1,0:T(8,128)(2,1)S(1)}, bf16[512,512]{1,0:T(8,128)(2,1)S(1)}, u32[]{:S(2)}, u32[]{:S(2)}) collective-permute-start(bf16[512,512]{1,0:T(8,128)(2,1)S(1)} %get-tuple-element.317), channel_id=1, source_target_pairs={{0,8},{8,16},{16,24},{1,9},{9,17},{17,25},{2,10},{10,18},{18,26},{... | collective-permute-start | bytes 1572872 | tf_op jit(solution)/shard_map/while/body/eval_jaxpr/ppermute | solution.py:12
  136.3 47.2 %all-gather.2.cloned.1.call-start = ((), (), s32[]{:S(2)}) async-start(), calls=%async_computation | async-start | bytes 4718592 | tf_op jit(solution)/shard_map/while/body/eval_jaxpr/all_gather | solution.py:38
  206.1 8.2 %copy-start = (bf16[512,4096]{1,0:T(8,128)(2,1)S(1)}, bf16[512,4096]{1,0:T(8,128)(2,1)}, u32[]{:S(2)}) copy-start(bf16[512,4096]{1,0:T(8,128)(2,1)} %all-gather.2.cloned.1.call-done) | copy-start | bytes 12582916 | tf_op jit(solution)/shard_map/while
  221.4 16.8 %collective-permute-start = (bf16[512,512]{1,0:T(8,128)(2,1)S(1)}, bf16[512,512]{1,0:T(8,128)(2,1)S(1)}, u32[]{:S(2)}, u32[]{:S(2)}) collective-permute-start(bf16[512,512]{1,0:T(8,128)(2,1)S(1)} %get-tuple-element.317), channel_id=1, source_target_pairs={{0,8},{8,16},{16,24},{1,9},{9,17},{17,25},{2,10},{10,18},{18,26},{... | collective-permute-start | bytes 1572872 | tf_op jit(solution)/shard_map/while/body/eval_jaxpr/ppermute | solution.py:12
  238.2 47.2 %all-gather.2.cloned.1.call-start = ((), (), s32[]{:S(2)}) async-start(), calls=%async_computation | async-start | bytes 4718592 | tf_op jit(solution)/shard_map/while/body/eval_jaxpr/all_gather | solution.py:38
  308.0 8.2 %copy-start = (bf16[512,4096]{1,0:T(8,128)(2,1)S(1)}, bf16[512,4096]{1,0:T(8,128)(2,1)}, u32[]{:S(2)}) copy-start(bf16[512,4096]{1,0:T(8,128)(2,1)} %all-gather.2.cloned.1.call-done) | copy-start | bytes 12582916 | tf_op jit(solution)/shard_map/while
  323.3 16.8 %collective-permute-start = (bf16[512,512]{1,0:T(8,128)(2,1)S(1)}, bf16[512,512]{1,0:T(8,128)(2,1)S(1)}, u32[]{:S(2)}, u32[]{:S(2)}) collective-permute-start(bf16[512,512]{1,0:T(8,128)(2,1)S(1)} %get-tuple-element.317), channel_id=1, source_target_pairs={{0,8},{8,16},{16,24},{1,9},{9,17},{17,25},{2,10},{10,18},{18,26},{... | collective-permute-start | bytes 1572872 | tf_op jit(solution)/shard_map/while/body/eval_jaxpr/ppermute | solution.py:12
  340.1 46.9 %all-gather.2.cloned.1.call-start = ((), (), s32[]{:S(2)}) async-start(), calls=%async_computation | async-start | bytes 4718592 | tf_op jit(solution)/shard_map/while/body/eval_jaxpr/all_gather | solution.py:38
  409.6 8.2 %copy-start = (bf16[512,4096]{1,0:T(8,128)(2,1)S(1)}, bf16[512,4096]{1,0:T(8,128)(2,1)}, u32[]{:S(2)}) copy-start(bf16[512,4096]{1,0:T(8,128)(2,1)} %all-gather.2.cloned.1.call-done) | copy-start | bytes 12582916 | tf_op jit(solution)/shard_map/while
  424.9 16.8 %collective-permute-start = (bf16[512,512]{1,0:T(8,128)(2,1)S(1)}, bf16[512,512]{1,0:T(8,128)(2,1)S(1)}, u32[]{:S(2)}, u32[]{:S(2)}) collective-permute-start(bf16[512,512]{1,0:T(8,128)(2,1)S(1)} %get-tuple-element.317), channel_id=1, source_target_pairs={{0,8},{8,16},{16,24},{1,9},{9,17},{17,25},{2,10},{10,18},{18,26},{... | collective-permute-start | bytes 1572872 | tf_op jit(solution)/shard_map/while/body/eval_jaxpr/ppermute | solution.py:12
  441.7 46.9 %all-gather.2.cloned.1.call-start = ((), (), s32[]{:S(2)}) async-start(), calls=%async_computation | async-start | bytes 4718592 | tf_op jit(solution)/shard_map/while/body/eval_jaxpr/all_gather | solution.py:38
  511.3 8.2 %copy-start = (bf16[512,4096]{1,0:T(8,128)(2,1)S(1)}, bf16[512,4096]{1,0:T(8,128)(2,1)}, u32[]{:S(2)}) copy-start(bf16[512,4096]{1,0:T(8,128)(2,1)} %all-gather.2.cloned.1.call-done) | copy-start | bytes 12582916 | tf_op jit(solution)/shard_map/while
  526.5 16.8 %collective-permute-start = (bf16[512,512]{1,0:T(8,128)(2,1)S(1)}, bf16[512,512]{1,0:T(8,128)(2,1)S(1)}, u32[]{:S(2)}, u32[]{:S(2)}) collective-permute-start(bf16[512,512]{1,0:T(8,128)(2,1)S(1)} %get-tuple-element.317), channel_id=1, source_target_pairs={{0,8},{8,16},{16,24},{1,9},{9,17},{17,25},{2,10},{10,18},{18,26},{... | collective-permute-start | bytes 1572872 | tf_op jit(solution)/shard_map/while/body/eval_jaxpr/ppermute | solution.py:12
  543.4 0.6 copy-start.3
Sparse Core Ops, SparseCore 0:
  33.5 48.0 all-gather.1
  138.7 44.7 all-gather.1
  240.6 44.7 all-gather.1
  342.2 44.7 all-gather.1
  443.9 44.7 all-gather.1
where the time goes:
time: 551 us
  waiting for transfers between devices  294 us (53%)
  matrix products  115 us (21%)
  local copies, waits for them, and re-layouts  66 us (12%)
  other arithmetic  45.2 us (8%)
  starting transfers between devices  16.9 us (3%)
  between operations  13.8 us (3%)
    all_gather x5, waiting for transfers between devices, tick(): piece = lax.all_gather(rows_in, 'bond', axis=1, tiled=True)  226 us
    dot_general x5, matrix products, tick(): total = jnp.dot(piece, a_mat, preferred_element_type=jnp.float32)  113 us
    ppermute x5, waiting for transfers between devices, shifted(): lax.ppermute(value, axis, [(source, source + steps) for source in range(i...  67.3 us
    while x15, local copies, waits for them, and re-layouts  40.9 us
    unnamed x9, local copies, waits for them, and re-layouts  23.3 us
    reduce_sum x5, other arithmetic, tick(): mixed = jnp.sum(weight[:, :, None] * prod, axis=1)  19.5 us
    ppermute x5, starting transfers between devices, shifted(): lax.ppermute(value, axis, [(source, source + steps) for source in range(i...  16.8 us
  transfers between devices with their start and end apart: 10, of which 10 were waited for; matrix products, arithmetic and copies ran while one was open for 0% of the time, Pallas kernels for 0%

commit v1 on v0

--- a/solution.py
+++ b/solution.py
@@ -35,7 +35,15 @@
         first = jnp.clip(batch, 0, ngroups - 1) * grows
         start_piece = lax.dynamic_slice_in_dim(start_rows, first, grows, 0)
         rows_in = jnp.where(position == 0, start_piece, incoming)
-        piece = lax.all_gather(rows_in, "bond", axis=1, tiled=True)
+        ways, here = (lax.axis_size("bond"), lax.axis_index("bond"))
+        grown, reach = (rows_in, 1)
+        while reach < ways:
+            theirs = lax.ppermute(grown, "bond", [(d, d ^ reach) for d in range(ways)])
+            mine_first = jnp.concatenate([grown, theirs], axis=1)
+            theirs_first = jnp.concatenate([theirs, grown], axis=1)
+            grown = jnp.where(here & reach == 0, mine_first, theirs_first)
+            reach = 2 * reach
+        piece = grown
         total = jnp.dot(piece, a_mat, preferred_element_type=jnp.float32)
         pf = piece.astype(jnp.float32)
         total, squares = (total, jnp.sum(pf * pf, axis=1))

time: 551 us -> 943 us (1.71)
  waiting for transfers between devices: 294 us -> 645 us
  other arithmetic: 45.2 us -> 68.1 us
  starting transfers between devices: 16.9 us -> 36 us
  between operations: 13.8 us -> 0.67 us
  matrix products: 115 us -> 126 us
    ppermute x0 -> x15, waiting for transfers between devices: none -> 578 us  [tick(): theirs = lax.ppermute(grown, 'bond', [(d, d ^ reach) for d in range(ways)])]
    all_gather x5 -> x0, waiting for transfers between devices: 226 us -> none  [tick(): piece = lax.all_gather(rows_in, 'bond', axis=1, tiled=True)]
    ppermute x0 -> x15, starting transfers between devices: none -> 24.4 us  [tick(): theirs = lax.ppermute(grown, 'bond', [(d, d ^ reach) for d in range(ways)])]
    reduce_sum x5, other arithmetic: 4.47 us -> 18.4 us  [tick(): total, squares = (total, jnp.sum(pf * pf, axis=1))]
    select_n x0 -> x10, other arithmetic: none -> 13.1 us  [tick(): grown = jnp.where(here & reach == 0, mine_first, theirs_first)]
    dot_general x5, matrix products: 113 us -> 124 us  [tick(): total = jnp.dot(piece, a_mat, preferred_element_type=jnp.float32)]
    while x15 -> x5, local copies, waits for them, and re-layouts: 40.9 us -> 40.5 us
  transfers between devices with their start and end apart: 10 -> 20, of which waited for: 10 -> 20; matrix products, arithmetic and copies ran while one was open for 0% -> 0% of each run, Pallas kernels for 0% -> 0%
where the time goes in v1:
time: 943 us; the launch traced here: 941 us
  waiting for transfers between devices  645 us (68%)
  matrix products  126 us (13%)
  other arithmetic  68.1 us (7%)
  local copies, waits for them, and re-layouts  65.7 us (7%)
  starting transfers between devices  36 us (4%)
    ppermute x15, waiting for transfers between devices, tick(): theirs = lax.ppermute(grown, 'bond', [(d, d ^ reach) for d in range(ways)])  578 us
    dot_general x5, matrix products, tick(): total = jnp.dot(piece, a_mat, preferred_element_type=jnp.float32)  124 us
    ppermute x5, waiting for transfers between devices, shifted(): lax.ppermute(value, axis, [(source, source + steps) for source in range(i...  66.9 us
    while x5, local copies, waits for them, and re-layouts  40.5 us
    ppermute x15, starting transfers between devices, tick(): theirs = lax.ppermute(grown, 'bond', [(d, d ^ reach) for d in range(ways)])  24.4 us
    unnamed x9, local copies, waits for them, and re-layouts  23.3 us
    reduce_sum x5, other arithmetic, tick(): mixed = jnp.sum(weight[:, :, None] * prod, axis=1)  19.5 us
  transfers between devices with their start and end apart: 20, of which 20 were waited for; matrix products, arithmetic and copies ran while one was open for 0% of the time, Pallas kernels for 0%

profile of v1, /device:TPU:4, one launch (start us, length us, event | category | flops | bytes accessed | tf_op | source)
XLA Modules:
  0.0 941.2 jit_solution(12995980864557633793)
XLA Ops:
  0.7 22.7 %copy.10 = bf16[512,8,8,512]{3,1,2,0:T(8,128)(2,1)} copy(bf16[512,8,8,512]{3,2,1,0:T(8,128)(2,1)} %bitcast.32) | data formatting | bytes 67108864
  24.5 916.1 %while.18 = (s32[]{:T(128)}, bf16[512,512]{1,0:T(8,128)(2,1)S(1)}, bf16[1024,512]{1,0:T(8,128)(2,1)}, f32[1024]{0:T(1024)S(1)}, s32[]{:T(128)}, /*index=5*/s32[1...) while((s32[]{:T(128)}, bf16[512,512]{1,0:T(8,128)(2,1)S(1)}, ...), condition=%wide.region_3.4_spmd, body=%wide.region_0.3_spmd.sunk | while | flops 17245542400 | bytes 103893904 | solution.py:75
  29.6 23.7 %collective-permute-done.1 = bf16[512,1024]{1,0:T(8,128)(2,1)} collective-permute-done((bf16[512,1024]{1,0:T(8,128)(2,1)S(1)}, bf16[512,1024]{1,0:T(8,128)(2,1)}, u32[]{:S(2)}, u32[]{:S(2)}) %collective-permute-start.1) | collective-permute-done | bytes 1048608 | tf_op jit(solution)/shard_map/while/body/eval_jaxpr/ppermute | solution.py:41
  58.8 89.7 %collective-permute-done.2 = bf16[512,2048]{1,0:T(8,128)(2,1)} collective-permute-done((bf16[512,2048]{1,0:T(8,128)(2,1)S(1)}, bf16[512,2048]{1,0:T(8,128)(2,1)}, u32[]{:S(2)}, u32[]{:S(2)}) %collective-permute-start.2) | collective-permute-done | bytes 2097184 | tf_op jit(solution)/shard_map/while/body/eval_jaxpr/ppermute | solution.py:41
  148.5 24.8 %fusion.16 = f32[512,4096]{1,0:T(8,128)S(1)} fusion(bf16[4096,4096]{1,0:T(8,128)(2,1)} %get-tuple-element.365, bf16[512,2048]{1,0:T(8,128)(2,1)} %collective-permute-done.2, bf16[512,2048]{1,0:T(8,128)(2,1)S(1)} %maximum_select_fusion.9, pred[]{:T(512)S(6)} %eq.86), kind=kOutput, calls=%fused_computation.8.clone.1 | convolution fusion | flops 17198743552 | bytes 46137344 | tf_op jit(solution)/shard_map/while/body/eval_jaxpr/dot_general | solution.py:47
  173.4 8.1 copy.12
  185.3 3.9 fusion.18
  194.7 12.2 %collective-permute-done.3 = bf16[512,512]{1,0:T(8,128)(2,1)S(1)} collective-permute-done((bf16[512,512]{1,0:T(8,128)(2,1)S(1)}, bf16[512,512]{1,0:T(8,128)(2,1)S(1)}, u32[]{:S(2)}, u32[]{:S(2)}) %collective-permute-start.3) | collective-permute-done | bytes 524320 | tf_op jit(solution)/shard_map/while/body/eval_jaxpr/ppermute | solution.py:12
  212.0 23.7 %collective-permute-done.1 = bf16[512,1024]{1,0:T(8,128)(2,1)} collective-permute-done((bf16[512,1024]{1,0:T(8,128)(2,1)S(1)}, bf16[512,1024]{1,0:T(8,128)(2,1)}, u32[]{:S(2)}, u32[]{:S(2)}) %collective-permute-start.1) | collective-permute-done | bytes 1048608 | tf_op jit(solution)/shard_map/while/body/eval_jaxpr/ppermute | solution.py:41
  242.0 89.9 %collective-permute-done.2 = bf16[512,2048]{1,0:T(8,128)(2,1)} collective-permute-done((bf16[512,2048]{1,0:T(8,128)(2,1)S(1)}, bf16[512,2048]{1,0:T(8,128)(2,1)}, u32[]{:S(2)}, u32[]{:S(2)}) %collective-permute-start.2) | collective-permute-done | bytes 2097184 | tf_op jit(solution)/shard_map/while/body/eval_jaxpr/ppermute | solution.py:41
  331.9 24.8 %fusion.16 = f32[512,4096]{1,0:T(8,128)S(1)} fusion(bf16[4096,4096]{1,0:T(8,128)(2,1)} %get-tuple-element.365, bf16[512,2048]{1,0:T(8,128)(2,1)} %collective-permute-done.2, bf16[512,2048]{1,0:T(8,128)(2,1)S(1)} %maximum_select_fusion.9, pred[]{:T(512)S(6)} %eq.86), kind=kOutput, calls=%fused_computation.8.clone.1 | convolution fusion | flops 17198743552 | bytes 46137344 | tf_op jit(solution)/shard_map/while/body/eval_jaxpr/dot_general | solution.py:47
  356.7 8.1 copy.12
  368.7 3.9 fusion.18
  377.2 13.2 %collective-permute-done.3 = bf16[512,512]{1,0:T(8,128)(2,1)S(1)} collective-permute-done((bf16[512,512]{1,0:T(8,128)(2,1)S(1)}, bf16[512,512]{1,0:T(8,128)(2,1)S(1)}, u32[]{:S(2)}, u32[]{:S(2)}) %collective-permute-start.3) | collective-permute-done | bytes 524320 | tf_op jit(solution)/shard_map/while/body/eval_jaxpr/ppermute | solution.py:12
  395.4 23.8 %collective-permute-done.1 = bf16[512,1024]{1,0:T(8,128)(2,1)} collective-permute-done((bf16[512,1024]{1,0:T(8,128)(2,1)S(1)}, bf16[512,1024]{1,0:T(8,128)(2,1)}, u32[]{:S(2)}, u32[]{:S(2)}) %collective-permute-start.1) | collective-permute-done | bytes 1048608 | tf_op jit(solution)/shard_map/while/body/eval_jaxpr/ppermute | solution.py:41
  425.4 89.9 %collective-permute-done.2 = bf16[512,2048]{1,0:T(8,128)(2,1)} collective-permute-done((bf16[512,2048]{1,0:T(8,128)(2,1)S(1)}, bf16[512,2048]{1,0:T(8,128)(2,1)}, u32[]{:S(2)}, u32[]{:S(2)}) %collective-permute-start.2) | collective-permute-done | bytes 2097184 | tf_op jit(solution)/shard_map/while/body/eval_jaxpr/ppermute | solution.py:41
  515.3 24.8 %fusion.16 = f32[512,4096]{1,0:T(8,128)S(1)} fusion(bf16[4096,4096]{1,0:T(8,128)(2,1)} %get-tuple-element.365, bf16[512,2048]{1,0:T(8,128)(2,1)} %collective-permute-done.2, bf16[512,2048]{1,0:T(8,128)(2,1)S(1)} %maximum_select_fusion.9, pred[]{:T(512)S(6)} %eq.86), kind=kOutput, calls=%fused_computation.8.clone.1 | convolution fusion | flops 17198743552 | bytes 46137344 | tf_op jit(solution)/shard_map/while/body/eval_jaxpr/dot_general | solution.py:47
  540.1 8.1 copy.12
  552.1 3.9 fusion.18
  560.0 13.8 %collective-permute-done.3 = bf16[512,512]{1,0:T(8,128)(2,1)S(1)} collective-permute-done((bf16[512,512]{1,0:T(8,128)(2,1)S(1)}, bf16[512,512]{1,0:T(8,128)(2,1)S(1)}, u32[]{:S(2)}, u32[]{:S(2)}) %collective-permute-start.3) | collective-permute-done | bytes 524320 | tf_op jit(solution)/shard_map/while/body/eval_jaxpr/ppermute | solution.py:12
  578.9 23.8 %collective-permute-done.1 = bf16[512,1024]{1,0:T(8,128)(2,1)} collective-permute-done((bf16[512,1024]{1,0:T(8,128)(2,1)S(1)}, bf16[512,1024]{1,0:T(8,128)(2,1)}, u32[]{:S(2)}, u32[]{:S(2)}) %collective-permute-start.1) | collective-permute-done | bytes 1048608 | tf_op jit(solution)/shard_map/while/body/eval_jaxpr/ppermute | solution.py:41
  608.8 89.9 %collective-permute-done.2 = bf16[512,2048]{1,0:T(8,128)(2,1)} collective-permute-done((bf16[512,2048]{1,0:T(8,128)(2,1)S(1)}, bf16[512,2048]{1,0:T(8,128)(2,1)}, u32[]{:S(2)}, u32[]{:S(2)}) %collective-permute-start.2) | collective-permute-done | bytes 2097184 | tf_op jit(solution)/shard_map/while/body/eval_jaxpr/ppermute | solution.py:41
  698.7 24.8 %fusion.16 = f32[512,4096]{1,0:T(8,128)S(1)} fusion(bf16[4096,4096]{1,0:T(8,128)(2,1)} %get-tuple-element.365, bf16[512,2048]{1,0:T(8,128)(2,1)} %collective-permute-done.2, bf16[512,2048]{1,0:T(8,128)(2,1)S(1)} %maximum_select_fusion.9, pred[]{:T(512)S(6)} %eq.86), kind=kOutput, calls=%fused_computation.8.clone.1 | convolution fusion | flops 17198743552 | bytes 46137344 | tf_op jit(solution)/shard_map/while/body/eval_jaxpr/dot_general | solution.py:47
  723.5 8.1 copy.12
  735.5 3.9 fusion.18
  743.4 13.8 %collective-permute-done.3 = bf16[512,512]{1,0:T(8,128)(2,1)S(1)} collective-permute-done((bf16[512,512]{1,0:T(8,128)(2,1)S(1)}, bf16[512,512]{1,0:T(8,128)(2,1)S(1)}, u32[]{:S(2)}, u32[]{:S(2)}) %collective-permute-start.3) | collective-permute-done | bytes 524320 | tf_op jit(solution)/shard_map/while/body/eval_jaxpr/ppermute | solution.py:12
  762.3 23.8 %collective-permute-done.1 = bf16[512,1024]{1,0:T(8,128)(2,1)} collective-permute-done((bf16[512,1024]{1,0:T(8,128)(2,1)S(1)}, bf16[512,1024]{1,0:T(8,128)(2,1)}, u32[]{:S(2)}, u32[]{:S(2)}) %collective-permute-start.1) | collective-permute-done | bytes 1048608 | tf_op jit(solution)/shard_map/while/body/eval_jaxpr/ppermute | solution.py:41
  792.2 89.9 %collective-permute-done.2 = bf16[512,2048]{1,0:T(8,128)(2,1)} collective-permute-done((bf16[512,2048]{1,0:T(8,128)(2,1)S(1)}, bf16[512,2048]{1,0:T(8,128)(2,1)}, u32[]{:S(2)}, u32[]{:S(2)}) %collective-permute-start.2) | collective-permute-done | bytes 2097184 | tf_op jit(solution)/shard_map/while/body/eval_jaxpr/ppermute | solution.py:41
  882.1 24.8 %fusion.16 = f32[512,4096]{1,0:T(8,128)S(1)} fusion(bf16[4096,4096]{1,0:T(8,128)(2,1)} %get-tuple-element.365, bf16[512,2048]{1,0:T(8,128)(2,1)} %collective-permute-done.2, bf16[512,2048]{1,0:T(8,128)(2,1)S(1)} %maximum_select_fusion.9, pred[]{:T(512)S(6)} %eq.86), kind=kOutput, calls=%fused_computation.8.clone.1 | convolution fusion | flops 17198743552 | bytes 46137344 | tf_op jit(solution)/shard_map/while/body/eval_jaxpr/dot_general | solution.py:47
  907.0 8.1 copy.12
  918.9 3.9 fusion.18
  926.8 13.8 %collective-permute-done.3 = bf16[512,512]{1,0:T(8,128)(2,1)S(1)} collective-permute-done((bf16[512,512]{1,0:T(8,128)(2,1)S(1)}, bf16[512,512]{1,0:T(8,128)(2,1)S(1)}, u32[]{:S(2)}, u32[]{:S(2)}) %collective-permute-start.3) | collective-permute-done | bytes 524320 | tf_op jit(solution)/shard_map/while/body/eval_jaxpr/ppermute | solution.py:12
  (81 shorter events, 98.1 us)
Async XLA Ops:
  0.6 23.9 %copy-start = (f32[1,8,8]{2,1,0:T(8,128)S(1)}, f32[1,8,8]{2,1,0:T(8,128)}, u32[]{:S(2)}) copy-start(f32[1,8,8]{2,1,0:T(8,128)} %param.10) | copy-start | bytes 772
  0.6 23.8 %copy-start.1 = (f32[1,8,4]{1,2,0:T(4,128)S(1)}, f32[1,8,4]{1,2,0:T(4,128)}, u32[]{:S(2)}) copy-start(f32[1,8,4]{1,2,0:T(4,128)} %param.9) | copy-start | bytes 388
  0.7 23.8 %copy-start.3 = (s32[1,1024]{1,0:T(1,128)S(1)}, s32[1,1024]{1,0:T(1,128)}, u32[]{:S(2)}) copy-start(s32[1,1024]{1,0:T(1,128)} %param.11) | copy-start | bytes 12292
  25.7 2.0 collective-permute-start
  28.0 25.4 %collective-permute-start.1 = (bf16[512,1024]{1,0:T(8,128)(2,1)S(1)}, bf16[512,1024]{1,0:T(8,128)(2,1)}, u32[]{:S(2)}, u32[]{:S(2)}) collective-permute-start(bf16[512,1024]{1,0:T(8,128)(2,1)S(1)} %maximum_select_fusion.8), channel_id=1, source_target_pairs={{0,2},{1,3},{2,0},{3,1},{4,6},{5,7},{6,4},{7,5},{8,10},{9,11},{10,... | collective-permute-start | bytes 3145736 | tf_op jit(solution)/shard_map/while/body/eval_jaxpr/ppermute | solution.py:41
  55.7 92.8 %collective-permute-start.2 = (bf16[512,2048]{1,0:T(8,128)(2,1)S(1)}, bf16[512,2048]{1,0:T(8,128)(2,1)}, u32[]{:S(2)}, u32[]{:S(2)}) collective-permute-start(bf16[512,2048]{1,0:T(8,128)(2,1)S(1)} %maximum_select_fusion.9), channel_id=1, source_target_pairs={{0,4},{1,5},{2,6},{3,7},{4,0},{5,1},{6,2},{7,3},{8,12},{9,13},{10,... | collective-permute-start | bytes 6291464 | tf_op jit(solution)/shard_map/while/body/eval_jaxpr/ppermute | solution.py:41
  191.3 15.6 %collective-permute-start.3 = (bf16[512,512]{1,0:T(8,128)(2,1)S(1)}, bf16[512,512]{1,0:T(8,128)(2,1)S(1)}, u32[]{:S(2)}, u32[]{:S(2)}) collective-permute-start(bf16[512,512]{1,0:T(8,128)(2,1)S(1)} %get-tuple-element.317), channel_id=1, source_target_pairs={{0,8},{8,16},{16,24},{1,9},{9,17},{17,25},{2,10},{10,18},{18,26},{... | collective-permute-start | bytes 1572872 | tf_op jit(solution)/shard_map/while/body/eval_jaxpr/ppermute | solution.py:12
  208.1 2.0 collective-permute-start
  210.4 25.4 %collective-permute-start.1 = (bf16[512,1024]{1,0:T(8,128)(2,1)S(1)}, bf16[512,1024]{1,0:T(8,128)(2,1)}, u32[]{:S(2)}, u32[]{:S(2)}) collective-permute-start(bf16[512,1024]{1,0:T(8,128)(2,1)S(1)} %maximum_select_fusion.8), channel_id=1, source_target_pairs={{0,2},{1,3},{2,0},{3,1},{4,6},{5,7},{6,4},{7,5},{8,10},{9,11},{10,... | collective-permute-start | bytes 3145736 | tf_op jit(solution)/shard_map/while/body/eval_jaxpr/ppermute | solution.py:41
  238.1 93.8 %collective-permute-start.2 = (bf16[512,2048]{1,0:T(8,128)(2,1)S(1)}, bf16[512,2048]{1,0:T(8,128)(2,1)}, u32[]{:S(2)}, u32[]{:S(2)}) collective-permute-start(bf16[512,2048]{1,0:T(8,128)(2,1)S(1)} %maximum_select_fusion.9), channel_id=1, source_target_pairs={{0,4},{1,5},{2,6},{3,7},{4,0},{5,1},{6,2},{7,3},{8,12},{9,13},{10,... | collective-permute-start | bytes 6291464 | tf_op jit(solution)/shard_map/while/body/eval_jaxpr/ppermute | solution.py:41
  374.7 15.7 %collective-permute-start.3 = (bf16[512,512]{1,0:T(8,128)(2,1)S(1)}, bf16[512,512]{1,0:T(8,128)(2,1)S(1)}, u32[]{:S(2)}, u32[]{:S(2)}) collective-permute-start(bf16[512,512]{1,0:T(8,128)(2,1)S(1)} %get-tuple-element.317), channel_id=1, source_target_pairs={{0,8},{8,16},{16,24},{1,9},{9,17},{17,25},{2,10},{10,18},{18,26},{... | collective-permute-start | bytes 1572872 | tf_op jit(solution)/shard_map/while/body/eval_jaxpr/ppermute | solution.py:12
  391.6 2.0 collective-permute-start
  393.9 25.4 %collective-permute-start.1 = (bf16[512,1024]{1,0:T(8,128)(2,1)S(1)}, bf16[512,1024]{1,0:T(8,128)(2,1)}, u32[]{:S(2)}, u32[]{:S(2)}) collective-permute-start(bf16[512,1024]{1,0:T(8,128)(2,1)S(1)} %maximum_select_fusion.8), channel_id=1, source_target_pairs={{0,2},{1,3},{2,0},{3,1},{4,6},{5,7},{6,4},{7,5},{8,10},{9,11},{10,... | collective-permute-start | bytes 3145736 | tf_op jit(solution)/shard_map/while/body/eval_jaxpr/ppermute | solution.py:41
  421.6 93.7 %collective-permute-start.2 = (bf16[512,2048]{1,0:T(8,128)(2,1)S(1)}, bf16[512,2048]{1,0:T(8,128)(2,1)}, u32[]{:S(2)}, u32[]{:S(2)}) collective-permute-start(bf16[512,2048]{1,0:T(8,128)(2,1)S(1)} %maximum_select_fusion.9), channel_id=1, source_target_pairs={{0,4},{1,5},{2,6},{3,7},{4,0},{5,1},{6,2},{7,3},{8,12},{9,13},{10,... | collective-permute-start | bytes 6291464 | tf_op jit(solution)/shard_map/while/body/eval_jaxpr/ppermute | solution.py:41
  558.1 15.7 %collective-permute-start.3 = (bf16[512,512]{1,0:T(8,128)(2,1)S(1)}, bf16[512,512]{1,0:T(8,128)(2,1)S(1)}, u32[]{:S(2)}, u32[]{:S(2)}) collective-permute-start(bf16[512,512]{1,0:T(8,128)(2,1)S(1)} %get-tuple-element.317), channel_id=1, source_target_pairs={{0,8},{8,16},{16,24},{1,9},{9,17},{17,25},{2,10},{10,18},{18,26},{... | collective-permute-start | bytes 1572872 | tf_op jit(solution)/shard_map/while/body/eval_jaxpr/ppermute | solution.py:12
  575.0 2.0 collective-permute-start
  577.3 25.4 %collective-permute-start.1 = (bf16[512,1024]{1,0:T(8,128)(2,1)S(1)}, bf16[512,1024]{1,0:T(8,128)(2,1)}, u32[]{:S(2)}, u32[]{:S(2)}) collective-permute-start(bf16[512,1024]{1,0:T(8,128)(2,1)S(1)} %maximum_select_fusion.8), channel_id=1, source_target_pairs={{0,2},{1,3},{2,0},{3,1},{4,6},{5,7},{6,4},{7,5},{8,10},{9,11},{10,... | collective-permute-start | bytes 3145736 | tf_op jit(solution)/shard_map/while/body/eval_jaxpr/ppermute | solution.py:41
  605.0 93.7 %collective-permute-start.2 = (bf16[512,2048]{1,0:T(8,128)(2,1)S(1)}, bf16[512,2048]{1,0:T(8,128)(2,1)}, u32[]{:S(2)}, u32[]{:S(2)}) collective-permute-start(bf16[512,2048]{1,0:T(8,128)(2,1)S(1)} %maximum_select_fusion.9), channel_id=1, source_target_pairs={{0,4},{1,5},{2,6},{3,7},{4,0},{5,1},{6,2},{7,3},{8,12},{9,13},{10,... | collective-permute-start | bytes 6291464 | tf_op jit(solution)/shard_map/while/body/eval_jaxpr/ppermute | solution.py:41
  741.5 15.7 %collective-permute-start.3 = (bf16[512,512]{1,0:T(8,128)(2,1)S(1)}, bf16[512,512]{1,0:T(8,128)(2,1)S(1)}, u32[]{:S(2)}, u32[]{:S(2)}) collective-permute-start(bf16[512,512]{1,0:T(8,128)(2,1)S(1)} %get-tuple-element.317), channel_id=1, source_target_pairs={{0,8},{8,16},{16,24},{1,9},{9,17},{17,25},{2,10},{10,18},{18,26},{... | collective-permute-start | bytes 1572872 | tf_op jit(solution)/shard_map/while/body/eval_jaxpr/ppermute | solution.py:12
  758.4 2.0 collective-permute-start
  760.7 25.4 %collective-permute-start.1 = (bf16[512,1024]{1,0:T(8,128)(2,1)S(1)}, bf16[512,1024]{1,0:T(8,128)(2,1)}, u32[]{:S(2)}, u32[]{:S(2)}) collective-permute-start(bf16[512,1024]{1,0:T(8,128)(2,1)S(1)} %maximum_select_fusion.8), channel_id=1, source_target_pairs={{0,2},{1,3},{2,0},{3,1},{4,6},{5,7},{6,4},{7,5},{8,10},{9,11},{10,... | collective-permute-start | bytes 3145736 | tf_op jit(solution)/shard_map/while/body/eval_jaxpr/ppermute | solution.py:41
  788.4 93.7 %collective-permute-start.2 = (bf16[512,2048]{1,0:T(8,128)(2,1)S(1)}, bf16[512,2048]{1,0:T(8,128)(2,1)}, u32[]{:S(2)}, u32[]{:S(2)}) collective-permute-start(bf16[512,2048]{1,0:T(8,128)(2,1)S(1)} %maximum_select_fusion.9), channel_id=1, source_target_pairs={{0,4},{1,5},{2,6},{3,7},{4,0},{5,1},{6,2},{7,3},{8,12},{9,13},{10,... | collective-permute-start | bytes 6291464 | tf_op jit(solution)/shard_map/while/body/eval_jaxpr/ppermute | solution.py:41
  924.9 15.7 %collective-permute-start.3 = (bf16[512,512]{1,0:T(8,128)(2,1)S(1)}, bf16[512,512]{1,0:T(8,128)(2,1)S(1)}, u32[]{:S(2)}, u32[]{:S(2)}) collective-permute-start(bf16[512,512]{1,0:T(8,128)(2,1)S(1)} %get-tuple-element.317), channel_id=1, source_target_pairs={{0,8},{8,16},{16,24},{1,9},{9,17},{17,25},{2,10},{10,18},{18,26},{... | collective-permute-start | bytes 1572872 | tf_op jit(solution)/shard_map/while/body/eval_jaxpr/ppermute | solution.py:12
  940.6 0.6 copy-start.2
